TPU v7x, 256 devices: a whole 4x4x8 slice. The times are simulated.
256 devices in a mesh: gx: 16 (over y_lo, x, core), ch: 16 (over z, y_hi).
Axes of the slice: x: 4, y: 4 (y_hi: 2, y_lo: 2; y = y_hi * 2 + y_lo), z: 8, core: 2. Of those that a mesh axis runs over, the one named last changes fastest.
Arguments:
- activations: bfloat16 [128, 256, 4, 128], P('ch', 'gx'), may hold values from -6 to 6
- conv_weight: bfloat16 [27, 128, 128], P(None, None, 'ch'), may hold values from -0.109375 to 0.109375
- out_grad: bfloat16 [128, 256, 4, 128], P('ch', 'gx'), may hold values from -6 to 6
Outputs:
- features_out: bfloat16 [128, 256, 4, 128], P('ch', 'gx')
- input_grad: bfloat16 [128, 256, 4, 128], P('ch', 'gx')
All inputs are finite; a program needn't handle non-finite values.
Results may differ from a plain program's by a relative error of at most 0.001.
Values may be sent and summed in bfloat16 or wider, within the bound.
No kernel may reach another device: no remote copies, remote signals or barrier semaphores. Data moves between devices by JAX's collectives and lax.ppermute only.
A program may use at most 64 MiB of HBM per device.

v0:
```python
import jax
import jax.numpy as jnp
from jax import lax
from jax.sharding import PartitionSpec as P


def with_halo(cells, sides, width):
    for axis, dim in sides:
        count = lax.axis_size(axis)
        head = lax.slice_in_dim(cells, 0, width, axis=dim)
        tail = lax.slice_in_dim(cells, cells.shape[dim] - width, cells.shape[dim], axis=dim)
        cells = jnp.concatenate(
            [
                lax.ppermute(tail, axis, [(i, (i + 1) % count) for i in range(count)]),
                cells,
                lax.ppermute(head, axis, [((i + 1) % count, i) for i in range(count)]),
            ],
            axis=dim,
        )
    return cells


def tap_sum(extended, weight, direction, pattern):
    planes = extended.shape[1] - 2
    depth = extended.shape[2]
    height = extended.shape[3]
    padded = jnp.pad(extended, ((0, 0), (0, 0), (1, 1), (1, 1)))
    summed = None
    for first in range(3):
        for second in range(3):
            for third in range(3):
                offset_x = 1 + direction * (first - 1)
                offset_y = 1 + direction * (second - 1)
                offset_z = 1 + direction * (third - 1)
                window_part = padded[
                    :,
                    offset_x : offset_x + planes,
                    offset_z : offset_z + depth,
                    offset_y : offset_y + height,
                ]
                product = jnp.einsum(
                    pattern,
                    window_part,
                    weight[9 * first + 3 * second + third],
                    preferred_element_type=jnp.float32,
                )
                summed = product if summed is None else summed + product
    return summed


def slab_faces(field):
    return with_halo(field, (("gx", 1),), 1)


def local(activations, conv_weight, out_grad):
    full_weight = lax.all_gather(conv_weight, "ch", axis=2, tiled=True)
    local_rows = activations.shape[0]
    extended_act = slab_faces(activations)
    sliced = conv_weight
    features_out = tap_sum(
        lax.all_gather(extended_act, "ch", axis=0, tiled=True), sliced, 1, "kxzy,kn->nxzy"
    ).astype(jnp.bfloat16)
    extended_grad = slab_faces(out_grad)
    own_start = lax.axis_index("ch") * local_rows
    weight_rows = lax.dynamic_slice_in_dim(full_weight, own_start, local_rows, 1)
    sliced = weight_rows
    input_grad = tap_sum(
        lax.all_gather(extended_grad, "ch", axis=0, tiled=True), sliced, -1, "kxzy,nk->nxzy"
    ).astype(jnp.bfloat16)
    return (features_out, input_grad)


def solution(mesh):
    return jax.shard_map(
        local,
        mesh=mesh,
        in_specs=(P("ch", "gx", None, None), P(None, None, "ch"), P("ch", "gx", None, None)),
        out_specs=(P("ch", "gx", None, None), P("ch", "gx", None, None)),
        check_vma=False,
    )
```

profile of v0, /device:TPU:2, one launch (start us, length us, event | category | flops | bytes accessed | tf_op | source)
XLA Modules:
  0.0 219.0 jit_solution(10602987286998030668)
XLA Ops:
  7.2 1.0 copy.18
  8.3 1.7 collective-permute-start.3
  10.0 1.3 collective-permute-done.2
  11.4 0.7 pad_maximum_fusion.1
  12.2 1.0 copy.14
  13.2 1.6 collective-permute-start
  15.0 1.3 collective-permute-done
  16.4 0.7 pad_maximum_fusion
  17.1 53.9 %all_gather.10 = bf16[27,128,128]{1,2,0:T(8,128)(2,1)S(1)} all-gather(bf16[27,128,8]{1,2,0:T(8,128)(2,1)} %param.4), channel_id=1, replica_groups=mesh['gx'=16,'ch'=16] {'ch'}, dimensions={2}, use_global_device_ids=true | all-gather | bytes 940032 | tf_op jit(solution)/shard_map/all_gather | solution.py:56
  71.0 36.9 %all-gather.5.cloned.1.call-done = bf16[128,18,4,128]{3,0,2,1:T(8,128)(2,1)} async-done(((bf16[8,18,4,128]{3,0,2,1:T(8,128)(2,1)}), bf16[128,18,4,128]{3,0,2,1:T(8,128)(2,1)}) %all-gather.5.cloned.1.call-update) | async-done | bytes 2359312 | tf_op jit(solution)/shard_map/all_gather | solution.py:68
  107.9 2.1 fusion.10
  110.7 0.8 fusion.12
  112.7 0.8 fusion.15
  115.2 0.7 fusion.19
  115.8 0.8 fusion.20
  117.9 0.8 fusion.23
  120.4 0.7 fusion.27
  121.0 0.8 fusion.28
  122.5 0.8 fusion.7
  124.4 0.7 fusion
  126.2 0.8 fusion.116
  127.0 0.7 copy.22
  127.7 66.4 %all-gather.3.cloned.1.call-done = bf16[128,18,4,128]{3,0,2,1:T(8,128)(2,1)} async-done(((bf16[8,18,4,128]{3,0,2,1:T(8,128)(2,1)}), bf16[128,18,4,128]{3,0,2,1:T(8,128)(2,1)}) %all-gather.3.cloned.1.call-update) | async-done | bytes 2359312 | tf_op jit(solution)/shard_map/all_gather | solution.py:61
  194.2 2.1 fusion.158
  196.8 0.7 fusion.31
  199.5 0.7 fusion.36
  201.4 0.7 fusion.39
  204.1 0.7 fusion.44
  206.2 0.7 fusion.60
  208.1 1.0 fusion.55
  209.7 0.7 fusion.107
  211.4 0.7 copy.21
  (51 shorter events, 19.9 us)
Async XLA Ops:
  7.2 100.7 %all-gather.5.cloned.1.call-start = ((), (), s32[]{:S(2)}) async-start(), calls=%async_computation.1 | async-start | bytes 2506752 | tf_op jit(solution)/shard_map/all_gather | solution.py:68
  8.2 3.2 %collective-permute-start.2 = (bf16[8,1,4,128]{3,0,2,1:T(8,128)(2,1)S(1)}, bf16[8,1,4,128]{3,0,2,1:T(8,128)(2,1)S(1)}, u32[]{:S(2)}, u32[]{:S(2)}) collective-permute-start(bf16[8,1,4,128]{3,0,2,1:T(8,128)(2,1)S(1)} %get-tuple-element.6), channel_id=1, source_target_pairs={{0,16},{16,32},{32,48},{48,64},{64,80},{80,96},{96,112},{112,128},... | collective-permute-start | bytes 24584 | tf_op jit(solution)/shard_map/ppermute | solution.py:14
  8.3 3.1 %collective-permute-start.3 = (bf16[8,1,4,128]{3,0,2,1:T(8,128)(2,1)S(1)}, bf16[8,1,4,128]{3,0,2,1:T(8,128)(2,1)S(1)}, u32[]{:S(2)}, u32[]{:S(2)}) collective-permute-start(bf16[8,1,4,128]{3,0,2,1:T(8,128)(2,1)S(1)} %get-tuple-element.7), channel_id=1, source_target_pairs={{16,0},{32,16},{48,32},{64,48},{80,64},{96,80},{112,96},{128,112},... | collective-permute-start | bytes 24584 | tf_op jit(solution)/shard_map/ppermute | solution.py:16
  12.1 182.1 %all-gather.3.cloned.1.call-start = ((), (), s32[]{:S(2)}) async-start(), calls=%async_computation | async-start | bytes 2506752 | tf_op jit(solution)/shard_map/all_gather | solution.py:61
  13.2 3.2 %collective-permute-start = (bf16[8,1,4,128]{3,0,2,1:T(8,128)(2,1)S(1)}, bf16[8,1,4,128]{3,0,2,1:T(8,128)(2,1)S(1)}, u32[]{:S(2)}, u32[]{:S(2)}) collective-permute-start(bf16[8,1,4,128]{3,0,2,1:T(8,128)(2,1)S(1)} %get-tuple-element.8), channel_id=1, source_target_pairs={{0,16},{16,32},{32,48},{48,64},{64,80},{80,96},{96,112},{112,128},... | collective-permute-start | bytes 24584 | tf_op jit(solution)/shard_map/ppermute | solution.py:14
  14.8 1.6 collective-permute-start.1
  107.9 2.1 copy-start.1
  126.2 68.0 %copy-start.2 = (bf16[27,128,8]{1,2,0:T(8,128)(2,1)S(1)}, bf16[27,128,8]{1,2,0:T(8,128)(2,1)}, u32[]{:S(2)}) copy-start(bf16[27,128,8]{1,2,0:T(8,128)(2,1)} %param.4) | copy-start | bytes 165892
  194.2 2.3 %copy-start = (bf16[128,18,4,128]{3,0,2,1:T(8,128)(2,1)S(1)}, bf16[128,18,4,128]{3,0,2,1:T(8,128)(2,1)}, u32[]{:S(2)}) copy-start(bf16[128,18,4,128]{3,0,2,1:T(8,128)(2,1)} %all-gather.3.cloned.1.call-done) | copy-start | bytes 7077892
Sparse Core Ops, SparseCore 0:
  12.2 95.5 all-gather.4
  110.3 83.7 all-gather.2
where the time goes:
time: 219 us
  waiting for transfers between devices  106 us (48%)
  blocking collectives  53.9 us (25%)
  matrix products  36.1 us (16%)
  between operations  14.1 us (6%)
  starting transfers between devices  3.77 us (2%)
  local copies, waits for them, and re-layouts  3.68 us (2%)
    all_gather x1, waiting for transfers between devices, local(): lax.all_gather(extended_act, 'ch', axis=0, tiled=True)  66.4 us
    all_gather x1, blocking collectives, local(): full_weight = lax.all_gather(conv_weight, 'ch', axis=2, tiled=True)  53.9 us
    all_gather x1, waiting for transfers between devices, local(): lax.all_gather(extended_grad, 'ch', axis=0, tiled=True)  36.9 us
    dot_general x54, matrix products, tap_sum(): jnp.einsum(pattern, window_part, weight[9 * first + 3 * second + third],...  36.1 us
  transfers between devices with their start and end apart: 6, of which 5 were waited for; matrix products, arithmetic and copies ran while one was open for 10% of the time, Pallas kernels for 0%

commit v1 on v0

--- a/solution.py
+++ b/solution.py
@@ -2,6 +2,13 @@
 import jax.numpy as jnp
 from jax import lax
 from jax.sharding import PartitionSpec as P
+
+
+def all_by_exchange(block, axis, dim):
+    n_dev = lax.axis_size(axis)
+    pieces = jnp.stack([block for _ in range(n_dev)])
+    pieces = lax.all_to_all(pieces, axis, split_axis=0, concat_axis=0)
+    return jnp.concatenate(pieces, axis=dim)
 
 
 def with_halo(cells, sides, width):
@@ -58,7 +65,7 @@
     extended_act = slab_faces(activations)
     sliced = conv_weight
     features_out = tap_sum(
-        lax.all_gather(extended_act, "ch", axis=0, tiled=True), sliced, 1, "kxzy,kn->nxzy"
+        all_by_exchange(extended_act, "ch", 0), sliced, 1, "kxzy,kn->nxzy"
     ).astype(jnp.bfloat16)
     extended_grad = slab_faces(out_grad)
     own_start = lax.axis_index("ch") * local_rows

time: 219 us -> 192 us (0.88)
  waiting for transfers between devices: 106 us -> 16.6 us
  blocking collectives: 53.9 us -> 103 us
  starting transfers between devices: 3.77 us -> 15.3 us
    all_gather x1 -> x0, waiting for transfers between devices: 66.4 us -> none  [local(): lax.all_gather(extended_act, 'ch', axis=0, tiled=True)]
    all_gather x1, blocking collectives: 53.9 us -> 103 us  [local(): full_weight = lax.all_gather(conv_weight, 'ch', axis=2, tiled=True)]
    all_gather x1, waiting for transfers between devices: 36.9 us -> 13.9 us  [local(): lax.all_gather(extended_grad, 'ch', axis=0, tiled=True)]
    all_to_all x0 -> x1, starting transfers between devices: none -> 11.6 us  [all_by_exchange(): pieces = lax.all_to_all(pieces, axis, split_axis=0, concat_axis=0)]
  transfers between devices with their start and end apart: 6 -> 6, of which waited for: 5 -> 4; matrix products, arithmetic and copies ran while one was open for 10% -> 12% of each run, Pallas kernels for 0% -> 0%
where the time goes in v1:
time: 192 us; the launch traced here: 191 us
  blocking collectives  103 us (54%)
  matrix products  34.3 us (18%)
  waiting for transfers between devices  16.6 us (9%)
  starting transfers between devices  15.3 us (8%)
  between operations  14.1 us (7%)
  local copies, waits for them, and re-layouts  5.78 us (3%)
    all_gather x1, blocking collectives, local(): full_weight = lax.all_gather(conv_weight, 'ch', axis=2, tiled=True)  103 us
    dot_general x54, matrix products, tap_sum(): jnp.einsum(pattern, window_part, weight[9 * first + 3 * second + third],...  34.3 us
    all_gather x1, waiting for transfers between devices, local(): lax.all_gather(extended_grad, 'ch', axis=0, tiled=True)  13.9 us
    all_to_all x1, starting transfers between devices, all_by_exchange(): pieces = lax.all_to_all(pieces, axis, split_axis=0, concat_axis=0)  11.6 us
  transfers between devices with their start and end apart: 6, of which 4 were waited for; matrix products, arithmetic and copies ran while one was open for 12% of the time, Pallas kernels for 0%

profile of v1, /device:TPU:2, one launch (start us, length us, event | category | flops | bytes accessed | tf_op | source)
XLA Modules:
  0.0 190.5 jit_solution(2713305891705698201)
XLA Ops:
  7.2 1.0 copy.15
  8.3 1.7 collective-permute-start.3
  10.0 1.3 collective-permute-done.2
  11.4 0.7 pad_maximum_fusion.1
  12.1 0.7 fusion.250
  12.8 1.6 collective-permute-start
  14.7 1.3 collective-permute-done
  16.1 1.0 pad_maximum_fusion
  17.1 1.9 stack.2
  19.0 11.6 %all-to-all-start = ((bf16[16,8,18,4,128]{4,1,3,2,0:T(8,128)(2,1)}), bf16[16,8,18,4,128]{4,1,3,2,0:T(8,128)(2,1)S(1)}, u32[]{:S(2)}, u32[]{:S(2)}) async-start(bf16[16,8,18,4,128]{4,1,3,2,0:T(8,128)(2,1)} %stack.2), calls=%async_computation | async-start | bytes 4718592 | tf_op jit(solution)/shard_map/all_to_all | solution.py:10
  30.6 102.6 %all_gather.6 = bf16[27,128,128]{1,2,0:T(8,128)(2,1)S(1)} all-gather(bf16[27,128,8]{1,2,0:T(8,128)(2,1)S(1)} %copy-done.1), channel_id=1, replica_groups=mesh['gx'=16,'ch'=16] {'ch'}, dimensions={2}, use_global_device_ids=true | all-gather | bytes 940032 | tf_op jit(solution)/shard_map/all_gather | solution.py:63
  133.3 13.9 %all-gather.2.cloned.1.call-done = bf16[128,18,4,128]{3,0,2,1:T(8,128)(2,1)} async-done(((bf16[8,18,4,128]{3,0,2,1:T(8,128)(2,1)}), bf16[128,18,4,128]{3,0,2,1:T(8,128)(2,1)}) %all-gather.2.cloned.1.call-update) | async-done | bytes 2359312 | tf_op jit(solution)/shard_map/all_gather | solution.py:75
  147.1 2.1 %fusion.10 = f32[8,16,4,128]{3,0,2,1:T(8,128)S(1)} fusion(bf16[128,18,4,128]{3,0,2,1:T(8,128)(2,1)} %all-gather.2.cloned.1.call-done, bf16[27,128,128]{1,2,0:T(8,128)(2,1)S(1)} %all_gather.6, s32[]{:T(128)S(6)} %add.239, s32[]{:T(128)S(6)} %select_n.3), kind=kOutput, calls=%fused_computation.59 | convolution fusion | flops 16777216 | bytes 2654216 | tf_op jit(solution)/shard_map/kxzy,nk->nxzy/dot_general | solution.py:48
  149.9 0.8 fusion.12
  152.0 0.8 fusion.15
  154.5 0.7 fusion.19
  155.1 0.8 fusion.20
  157.2 0.8 fusion.23
  160.3 0.8 fusion.28
  161.7 0.8 fusion.7
  163.7 0.7 fusion
  165.4 0.8 fusion.116
  166.3 0.7 copy.19
  167.0 0.7 copy.106
  168.3 0.7 fusion.86
  171.4 0.7 fusion.81
  173.3 0.7 fusion.78
  176.4 0.7 fusion.73
  178.3 0.7 fusion.65
  179.0 0.9 fusion.66
  181.7 0.7 fusion.70
  183.0 0.7 copy.18
  (50 shorter events, 20.7 us)
Async XLA Ops:
  7.2 140.0 %all-gather.2.cloned.1.call-start = ((), (), s32[]{:S(2)}) async-start(), calls=%async_computation.1 | async-start | bytes 2506752 | tf_op jit(solution)/shard_map/all_gather | solution.py:75
  8.2 3.2 %collective-permute-start.2 = (bf16[8,1,4,128]{3,0,2,1:T(8,128)(2,1)S(1)}, bf16[8,1,4,128]{3,0,2,1:T(8,128)(2,1)S(1)}, u32[]{:S(2)}, u32[]{:S(2)}) collective-permute-start(bf16[8,1,4,128]{3,0,2,1:T(8,128)(2,1)S(1)} %get-tuple-element.6), channel_id=1, source_target_pairs={{0,16},{16,32},{32,48},{48,64},{64,80},{80,96},{96,112},{112,128},... | collective-permute-start | bytes 24584 | tf_op jit(solution)/shard_map/ppermute | solution.py:21
  8.3 3.1 %collective-permute-start.3 = (bf16[8,1,4,128]{3,0,2,1:T(8,128)(2,1)S(1)}, bf16[8,1,4,128]{3,0,2,1:T(8,128)(2,1)S(1)}, u32[]{:S(2)}, u32[]{:S(2)}) collective-permute-start(bf16[8,1,4,128]{3,0,2,1:T(8,128)(2,1)S(1)} %get-tuple-element.7), channel_id=1, source_target_pairs={{16,0},{32,16},{48,32},{64,48},{80,64},{96,80},{112,96},{128,112},... | collective-permute-start | bytes 24584 | tf_op jit(solution)/shard_map/ppermute | solution.py:23
  12.8 3.1 %collective-permute-start = (bf16[8,1,4,128]{3,2,1,0:T(4,128)(2,1)S(1)}, bf16[8,1,4,128]{3,2,1,0:T(4,128)(2,1)S(1)}, u32[]{:S(2)}, u32[]{:S(2)}) collective-permute-start(bf16[8,1,4,128]{3,2,1,0:T(4,128)(2,1)S(1)} %get-tuple-element.8), channel_id=1, source_target_pairs={{0,16},{16,32},{32,48},{48,64},{64,80},{80,96},{96,112},{112,128},... | collective-permute-start | bytes 24584 | tf_op jit(solution)/shard_map/ppermute | solution.py:21
  14.5 1.6 collective-permute-start.1
  19.0 11.6 %copy-start.1 = (bf16[27,128,8]{1,2,0:T(8,128)(2,1)S(1)}, bf16[27,128,8]{1,2,0:T(8,128)(2,1)}, u32[]{:S(2)}) copy-start(bf16[27,128,8]{1,2,0:T(8,128)(2,1)} %param.4) | copy-start | bytes 165892
  19.0 148.0 %all-to-all-start = ((bf16[16,8,18,4,128]{4,1,3,2,0:T(8,128)(2,1)}), bf16[16,8,18,4,128]{4,1,3,2,0:T(8,128)(2,1)S(1)}, u32[]{:S(2)}, u32[]{:S(2)}) async-start(bf16[16,8,18,4,128]{4,1,3,2,0:T(8,128)(2,1)} %stack.2), calls=%async_computation | async-start | bytes 4718592 | tf_op jit(solution)/shard_map/all_to_all | solution.py:10
  147.1 2.1 %copy-start = (bf16[128,18,4,128]{3,0,2,1:T(8,128)(2,1)S(1)}, bf16[128,18,4,128]{3,0,2,1:T(8,128)(2,1)}, u32[]{:S(2)}) copy-start(bf16[128,18,4,128]{3,0,2,1:T(8,128)(2,1)} %all-gather.2.cloned.1.call-done) | copy-start | bytes 7077892
Sparse Core Ops, SparseCore 0:
  12.2 134.8 all-gather.1
